TPU v7x, 32 devices: a whole 2x2x4 slice. The times are simulated.
32 devices in a mesh: shot: 2 (over y), row: 4 (over x, core), freq: 4 (over z).
Axes of the slice: x: 2, y: 2, z: 4, core: 2. Of those that a mesh axis runs over, the one named last changes fastest.
Arguments:
- source_field: float32 [2, 8, 1024, 1024], P(None, ('shot', 'freq'), 'row'), parts along dimension 1, may hold values from -6 to 6
- receiver_field: float32 [2, 8, 1024, 1024], P(None, ('shot', 'freq'), 'row'), parts along dimension 1, may hold values from -6 to 6
- slowness: float32 [4, 1024, 1024], P('freq', 'row'), may hold values from 0.22 to 0.67
- owner: int32 [4], replicated, may hold values from 0 to 3, each once
- freq_index: int32 [8], P(('shot', 'freq')), parts along dimension 0, may hold values from 0 to 3, each once
Outputs:
- source_out: float32 [2, 8, 1024, 1024], P(None, ('shot', 'freq'), 'row'), parts along dimension 1
- receiver_out: float32 [2, 8, 1024, 1024], P(None, ('shot', 'freq'), 'row'), parts along dimension 1
- image: float32 [4, 1024, 1024], P('shot', 'row', 'freq'), parts along dimension 0
There are 2 independent parts, one for each index of `shot`. A program takes and returns all parts, laid end to end along the dimension named above; an argument that names none is the same for every part. Nothing has to cross between parts.
All inputs are finite; a program needn't handle non-finite values.
Results may differ from a plain program's by a relative error of at most 0.00022.
Values sent between devices are 32-bit elements; how exact they have to be, the bound alone decides.
A program may use at most 128 MiB of HBM per device.

v0:
```python
import math
import jax
import jax.numpy as jnp
from jax import lax
from jax.sharding import PartitionSpec as P

NZ = 2
dz_km = 0.01
dx_km = 0.0125
ref_slow = 0.5
base_hertz = 3.0
step_hertz = 4.0
taper = 0.5


def spread(value, axis, source):
    kept = jnp.where(lax.axis_index(axis) == source, value, 0).astype(value.dtype)
    return lax.psum(kept, axis)


def split_length(length):
    return length // 128


def angle_table(count_a, count_b, modulus, sign):
    left = jnp.arange(count_a, dtype=jnp.int32)[:, None]
    right = jnp.arange(count_b, dtype=jnp.int32)[None, :]
    turns = (left * right % modulus).astype(jnp.float32) * (2.0 * math.pi / modulus)
    return (jnp.cos(turns), sign * jnp.sin(turns))


def contract(form, left, right):
    return jnp.einsum(form, left, right, precision=lax.Precision.HIGHEST)


def transform_pair(real_part, imag_part, sign, last):
    length = real_part.shape[2] if last else real_part.shape[1]
    first = split_length(length)
    second = length // first
    cos_a, sin_a = angle_table(first, first, first, sign)
    cos_b, sin_b = angle_table(second, second, second, sign)
    twist_c, twist_s = angle_table(first, second, length, sign)
    if last:
        shape = (real_part.shape[0], real_part.shape[1], first, second)
        form_one = "fajb,jk->fakb"
        form_two = "fakb,bm->famk"
    else:
        shape = (real_part.shape[0], first, second, real_part.shape[2])
        form_one = "fjbq,jk->fkbq"
        form_two = "fkbq,bm->fmkq"
        twist_c = twist_c[:, :, None]
        twist_s = twist_s[:, :, None]
    x_re = real_part.reshape(shape)
    x_im = imag_part.reshape(shape)
    y_re = contract(form_one, x_re, cos_a) - contract(form_one, x_im, sin_a)
    y_im = contract(form_one, x_im, cos_a) + contract(form_one, x_re, sin_a)
    z_re = y_re * twist_c - y_im * twist_s
    z_im = y_im * twist_c + y_re * twist_s
    out_re = contract(form_two, z_re, cos_b) - contract(form_two, z_im, sin_b)
    out_im = contract(form_two, z_im, cos_b) + contract(form_two, z_re, sin_b)
    return (out_re.reshape(real_part.shape), out_im.reshape(real_part.shape))


def transform(block, sign, last):
    count = block.shape[0]
    freqs = block.shape[2]
    plane = block.shape[3:]
    real_part = block[:, 0].reshape((count * freqs,) + plane)
    imag_part = block[:, 1].reshape((count * freqs,) + plane)
    out_re, out_im = transform_pair(real_part, imag_part, sign, last)
    shape = (count, freqs) + plane
    return jnp.stack([out_re.reshape(shape), out_im.reshape(shape)], axis=1)


def wavenumbers(length, start, count):
    index = start + jnp.arange(count, dtype=jnp.int32)
    signed = jnp.where(index * 2 < length, index, index - length)
    return signed.astype(jnp.float32) * (2.0 * math.pi / (length * dx_km))


def rotate(block, cos_v, sin_v):
    real_part = block[:, 0]
    imag_part = block[:, 1]
    return jnp.stack(
        [real_part * cos_v - imag_part * sin_v, imag_part * cos_v + real_part * sin_v], axis=1
    )


def shift_phase(block, omega, kx_part, ky_part, total):
    square = kx_part[:, None] ** 2 + ky_part[None, :] ** 2
    kmax = math.pi / dx_km
    damp = jnp.exp(-taper * square / (kmax * kmax)) / total
    ws0 = omega[:, None, None] * ref_slow
    vertical = ws0 - 0.5 * square[None] / ws0
    cos_v = jnp.cos(dz_km * vertical) * damp
    sin_v = jnp.sin(dz_km * vertical) * damp
    return rotate(block, cos_v, sin_v)


def correct(block, slab, omega):
    theta = omega[:, None, None] * (slab[None] - ref_slow) * dz_km
    return rotate(block, jnp.cos(theta), jnp.sin(theta))


def image_term(block):
    return jnp.sum(block[0, 0] * block[1, 0] - block[0, 1] * block[1, 1], axis=0)


def body(source_field, receiver_field, slowness, owner, freq_index):
    rows = source_field.shape[2]
    width = source_field.shape[3]
    row_count = lax.axis_size("row")
    height = rows * row_count
    cols = width // row_count
    place = lax.axis_index("row")
    omega = 2.0 * math.pi * (base_hertz + step_hertz * freq_index.astype(jnp.float32))
    mirrored = jnp.stack([receiver_field[0], -receiver_field[1]])
    fields = jnp.stack([source_field, mirrored])
    kx_all = wavenumbers(height, 0, height)
    ky_own = wavenumbers(width, place * cols, cols)
    total = float(height * width)
    slab_dev = slowness.shape[0]
    images = []
    for depth in range(NZ):
        chosen = owner[depth]
        held = spread(slowness, "freq", chosen // slab_dev)
        slab = lax.dynamic_index_in_dim(held, chosen % slab_dev, 0, keepdims=False)
        fields = transform(fields, -1.0, True)
        fields = lax.all_to_all(fields, "row", split_axis=4, concat_axis=3, tiled=True)
        items = fields
        items = transform(items, -1.0, False)
        items = shift_phase(items, omega, kx_all, ky_own, total)
        fields = transform(items, 1.0, False)
        fields = lax.all_to_all(fields, "row", split_axis=3, concat_axis=4, tiled=True)
        fields = transform(fields, 1.0, True)
        fields = correct(fields, slab, omega)
        images.append(image_term(fields))
    parts = [lax.psum_scatter(term, "freq", scatter_dimension=1, tiled=True) for term in images]
    image = jnp.stack(parts)
    source_out = fields[0]
    receiver_out = jnp.stack([fields[1, 0], -fields[1, 1]])
    return (source_out, receiver_out, image)


def solution(mesh):
    in_specs = (
        P(None, ("shot", "freq"), "row", None),
        P(None, ("shot", "freq"), "row", None),
        P("freq", "row", None),
        P(),
        P(("shot", "freq")),
    )
    out_specs = (
        P(None, ("shot", "freq"), "row", None),
        P(None, ("shot", "freq"), "row", None),
        P("shot", "row", "freq"),
    )
    return jax.shard_map(body, mesh=mesh, in_specs=in_specs, out_specs=out_specs, check_vma=False)
```

profile of v0, /device:TPU:0, one launch (start us, length us, event | category | flops | bytes accessed | tf_op | source)
XLA Modules:
  0.0 596.2 jit_solution(643073891319918496)
XLA Ops:
  20.3 2.7 fusion.112
  32.7 5.4 copy.346
  38.1 4.9 all-to-all-start
  44.0 4.0 fusion.186
  48.1 43.7 %all-to-all-done = f32[2,2,1,256,1024]{3,0,2,1,4:T(2,128)} async-done(((f32[2,2,1,256,1024]{3,0,2,1,4:T(2,128)}), f32[2,2,1,256,1024]{3,0,2,1,4:T(2,128)}, u32[]{:S(2)}, u32[]{:S(2)}) %all-to-all-start) | async-done | bytes 4194336 | tf_op jit(solution)/shard_map/all_to_all | solution.py:129
  91.8 5.0 copy.347
  96.7 5.4 copy.348
  104.7 2.9 fusion.104
  107.6 2.9 fusion.102
  110.5 2.9 fusion.118
  113.4 3.8 subtract_bitcast_fusion.13
  122.4 2.6 subtract_bitcast_fusion.12
  126.3 2.6 add_bitcast_fusion.12
  131.0 2.9 fusion.88
  133.9 2.9 fusion.86
  136.8 3.0 fusion.124
  139.8 3.9 subtract_bitcast_fusion.11
  143.7 2.6 fusion.80
  148.9 2.6 subtract_bitcast_fusion.10
  152.8 2.8 add_bitcast_fusion.10
  157.1 5.2 copy.372
  162.4 5.0 all-to-all-start.1
  171.0 90.0 %all-reduce.3.cloned.1.call-done = (f32[1,256,1024]{2,1,0:T(8,128)}, f32[1,256,1024]{2,1,0:T(8,128)}) async-done(((f32[1,256,1024]{2,1,0:T(8,128)}, f32[1,256,1024]{2,1,0:T(8,128)}), (f32[1,256,1024]{2,1,0:T(8,128)}, f32[1,256,1024]{2,1,0:T(8,128)})) %all-reduce.3.cloned.1.call-update) | async-done | bytes 2097168 | tf_op jit(solution)/shard_map/psum | solution.py:18
  260.9 4.7 fusion.192
  268.6 5.0 copy.373
  273.6 5.3 copy.374
  278.9 4.6 fusion.663
  285.6 3.2 fusion.318
  301.9 2.8 subtract_bitcast_fusion.8
  312.5 2.9 copy.386
  315.4 4.8 fusion.314
  320.2 3.1 copy.385
  323.3 3.6 fusion.316
  343.5 3.2 copy.395
  346.8 50.7 %all_to_all.72 = f32[2,2,1,256,1024]{3,0,2,1,4:T(2,128)S(1)} all-to-all(f32[2,2,1,256,1024]{3,0,2,1,4:T(2,128)S(1)} %copy.395), channel_id=1, replica_groups=mesh['shot'=2,'row'=4,'freq'=4] {'row'}, dimensions={4} | all-to-all | bytes 8388608 | tf_op jit(solution)/shard_map/all_to_all | solution.py:129
  397.5 2.7 copy.396
  400.3 5.7 copy.397
  408.5 2.9 fusion.56
  411.4 2.9 fusion.54
  414.3 2.9 fusion.130
  417.2 3.6 subtract_bitcast_fusion.5
  426.0 2.6 subtract_bitcast_fusion.4
  429.8 2.6 add_bitcast_fusion.4
  434.6 2.9 fusion.40
  437.5 2.9 fusion.38
  440.3 3.0 fusion.136
  443.4 4.0 subtract_bitcast_fusion.3
  447.4 2.6 fusion.32
  452.5 2.6 subtract_bitcast_fusion.2
  456.4 2.8 add_bitcast_fusion.2
  460.8 5.2 copy.418
  466.0 4.9 all-to-all-start.3
  471.0 2.6 copy.436
  474.9 5.7 cosine_bitcast_fusion
  484.7 4.7 fusion.10
  490.7 28.5 %all-to-all-done.3 = f32[2,2,1,1024,256]{4,0,2,1,3:T(2,128)} async-done(((f32[2,2,1,1024,256]{4,0,2,1,3:T(2,128)}), f32[2,2,1,1024,256]{4,0,2,1,3:T(2,128)}, u32[]{:S(2)}, u32[]{:S(2)}) %all-to-all-start.3) | async-done | bytes 4194336 | tf_op jit(solution)/shard_map/all_to_all | solution.py:134
  519.2 5.0 copy.419
  524.2 5.3 copy.420
  529.4 4.6 fusion.661
  536.1 3.2 fusion.306
  562.1 3.0 pad_maximum_fusion.6
  565.1 3.0 copy.444
  568.1 4.3 fusion.14
  574.3 13.1 %reduce-scatter.5.cloned.1.call-done = f32[256,256]{0,1:T(8,128)} async-done(((f32[256,1024]{0,1:T(8,128)}), f32[256,256]{0,1:T(8,128)}) %reduce-scatter.5.cloned.1.call-update) | async-done | bytes 262160 | tf_op jit(solution)/shard_map/reduce_scatter | solution.py:138
  (137 shorter events, 135.5 us)
Async XLA Ops:
  8.9 1.6 copy-start.19
  38.1 53.7 %all-to-all-start = ((f32[2,2,1,256,1024]{3,0,2,1,4:T(2,128)}), f32[2,2,1,256,1024]{3,0,2,1,4:T(2,128)}, u32[]{:S(2)}, u32[]{:S(2)}) async-start(f32[2,2,1,256,1024]{3,0,2,1,4:T(2,128)} %copy.346), calls=%async_computation | async-start | bytes 8388608 | tf_op jit(solution)/shard_map/all_to_all | solution.py:129
  48.1 82.2 %copy-start.8 = (f32[8,128,256]{2,1,0:T(8,128)}, f32[8,128,256]{2,1,0:T(8,128)S(1)}, u32[]{:S(2)}) copy-start(f32[8,128,256]{2,1,0:T(8,128)S(1)} %get-tuple-element.67) | copy-start | bytes 3145732
  162.4 5.1 copy-start.21
  162.4 7.0 %copy-start.20 = (f32[1,256,1024]{2,1,0:T(8,128)S(1)}, f32[1,256,1024]{2,1,0:T(8,128)}, u32[]{:S(2)}) copy-start(f32[1,256,1024]{2,1,0:T(8,128)} %param.7) | copy-start | bytes 3145732
  162.4 106.2 %all-to-all-start.1 = ((f32[2,2,1,1024,256]{4,0,2,1,3:T(2,128)}), f32[2,2,1,1024,256]{4,0,2,1,3:T(2,128)}, u32[]{:S(2)}, u32[]{:S(2)}) async-start(f32[2,2,1,1024,256]{4,0,2,1,3:T(2,128)} %copy.372), calls=%async_computation.1 | async-start | bytes 8388608 | tf_op jit(solution)/shard_map/all_to_all | solution.py:134
  167.4 93.5 %all-reduce.3.cloned.1.call-start = ((), (), s32[]{:S(2)}) async-start(), calls=%async_computation.8 | async-start | bytes 4194304 | tf_op jit(solution)/shard_map/psum | solution.py:18
  265.7 2.9 copy-start.11
  265.7 2.9 copy-start.13
  285.6 3.2 copy-start.6
  291.1 1.9 copy-start.14
  293.0 2.0 copy-start.7
  307.1 1.3 copy-start.1
  308.4 1.2 copy-start.17
  308.4 1.5 copy-start.18
  323.2 3.6 copy-start.2
  323.3 3.6 copy-start.15
  326.9 2.0 copy-start.5
  432.6 1.2 copy-start.9
  466.0 53.1 %all-to-all-start.3 = ((f32[2,2,1,1024,256]{4,0,2,1,3:T(2,128)}), f32[2,2,1,1024,256]{4,0,2,1,3:T(2,128)}, u32[]{:S(2)}, u32[]{:S(2)}) async-start(f32[2,2,1,1024,256]{4,0,2,1,3:T(2,128)} %copy.418), calls=%async_computation.3 | async-start | bytes 8388608 | tf_op jit(solution)/shard_map/all_to_all | solution.py:134
  470.9 2.7 copy-start.12
  470.9 103.4 %reduce-scatter.3.cloned.1.call-start = ((), (), s32[]{:S(2)}) async-start(), calls=%async_computation.6 | async-start | bytes 1310720 | tf_op jit(solution)/shard_map/reduce_scatter | solution.py:138
  490.7 96.8 %reduce-scatter.5.cloned.1.call-start = ((), (), s32[]{:S(2)}) async-start(), calls=%async_computation.7 | async-start | bytes 1310720 | tf_op jit(solution)/shard_map/reduce_scatter | solution.py:138
  536.1 3.2 copy-start.3
  541.8 1.9 copy-start.16
  543.7 2.0 copy-start.4
  555.2 2.3 copy-start.10
  557.5 2.5 copy-start
Sparse Core Ops, SparseCore 0:
  171.2 89.6 all-reduce.2
  490.8 26.5 reduce-scatter.2
  562.2 25.1 reduce-scatter.4
where the time goes:
time: 606 us; the launch traced here: 596 us
  waiting for transfers between devices  175 us (29%)
  matrix products  170 us (28%)
  local copies, waits for them, and re-layouts  125 us (21%)
  blocking collectives  50.7 us (8%)
  other arithmetic  42.9 us (7%)
  between operations  17.4 us (3%)
  starting transfers between devices  14.9 us (2%)
    dot_general x64, matrix products, contract(): return jnp.einsum(form, left, right, precision=lax.Precision.HIGHEST)  170 us
    psum x1, waiting for transfers between devices, spread(): return lax.psum(kept, axis)  90 us
    all_to_all x1, blocking collectives, body(): lax.all_to_all(fields, 'row', split_axis=4, concat_axis=3, tiled=True)  50.7 us
    all_to_all x1, waiting for transfers between devices, body(): lax.all_to_all(fields, 'row', split_axis=4, concat_axis=3, tiled=True)  43.7 us
    all_to_all x2, waiting for transfers between devices, body(): lax.all_to_all(fields, 'row', split_axis=3, concat_axis=4, tiled=True)  28.5 us
    all_to_all x4, local copies, waits for them, and re-layouts, body(): lax.all_to_all(fields, 'row', split_axis=3, concat_axis=4, tiled=True)  20.5 us
    another operation x4, local copies, waits for them, and re-layouts, transform(): return jnp.stack([out_re.reshape(shape), out_im.reshape(shape)], axis=1)  19.1 us
    all_to_all x4, local copies, waits for them, and re-layouts, body(): lax.all_to_all(fields, 'row', split_axis=4, concat_axis=3, tiled=True)  18.9 us
  transfers between devices with their start and end apart: 6, of which 4 were waited for; matrix products, arithmetic and copies ran while one was open for 15% of the time, Pallas kernels for 0%

commit v1 on v0

--- a/solution.py
+++ b/solution.py
@@ -13,9 +13,15 @@
 taper = 0.5
 
 
+def summed_here(array, name):
+    parts = lax.all_gather(array, name, axis=0, tiled=False)
+    result = parts.sum(axis=0)
+    return result
+
+
 def spread(value, axis, source):
     kept = jnp.where(lax.axis_index(axis) == source, value, 0).astype(value.dtype)
-    return lax.psum(kept, axis)
+    return summed_here(kept, axis)
 
 
 def split_length(length):

time: 606 us -> 580 us (0.957)
  waiting for transfers between devices: 175 us -> 145 us
  other arithmetic: 42.9 us -> 49.5 us
    psum x1 -> x0, waiting for transfers between devices: 90 us -> none  [spread(): return lax.psum(kept, axis)]
    all_to_all x2, waiting for transfers between devices: 28.5 us -> 87.5 us  [body(): lax.all_to_all(fields, 'row', split_axis=3, concat_axis=4, tiled=True)]
    mul x6 -> x0, local copies, waits for them, and re-layouts: 10.9 us -> none  [the longest x3 5.76 us: rotate(): real_part * cos_v - imag_part * sin_v]
    reduce_sum x0 -> x2, other arithmetic: none -> 7.38 us  [summed_here(): result = parts.sum(axis=0)]
  transfers between devices with their start and end apart: 6 -> 7, of which waited for: 4 -> 4; matrix products, arithmetic and copies ran while one was open for 15% -> 32% of each run, Pallas kernels for 0% -> 0%
where the time goes in v1:
time: 580 us; the launch traced here: 570 us
  matrix products  171 us (29%)
  waiting for transfers between devices  145 us (25%)
  local copies, waits for them, and re-layouts  122 us (21%)
  blocking collectives  50.7 us (9%)
  other arithmetic  49.5 us (9%)
  between operations  17.5 us (3%)
  starting transfers between devices  15 us (3%)
    dot_general x64, matrix products, contract(): return jnp.einsum(form, left, right, precision=lax.Precision.HIGHEST)  171 us
    all_to_all x2, waiting for transfers between devices, body(): lax.all_to_all(fields, 'row', split_axis=3, concat_axis=4, tiled=True)  87.5 us
    all_to_all x1, blocking collectives, body(): lax.all_to_all(fields, 'row', split_axis=4, concat_axis=3, tiled=True)  50.7 us
    all_to_all x1, waiting for transfers between devices, body(): lax.all_to_all(fields, 'row', split_axis=4, concat_axis=3, tiled=True)  40.2 us
    all_to_all x4, local copies, waits for them, and re-layouts, body(): lax.all_to_all(fields, 'row', split_axis=3, concat_axis=4, tiled=True)  20.5 us
    another operation x4, local copies, waits for them, and re-layouts, transform(): return jnp.stack([out_re.reshape(shape), out_im.reshape(shape)], axis=1)  19.4 us
    all_to_all x4, local copies, waits for them, and re-layouts, body(): lax.all_to_all(fields, 'row', split_axis=4, concat_axis=3, tiled=True)  18.8 us
    reduce_scatter x2, waiting for transfers between devices, body(): lax.psum_scatter(term, 'freq', scatter_dimension=1, tiled=True)  16 us
  transfers between devices with their start and end apart: 7, of which 4 were waited for; matrix products, arithmetic and copies ran while one was open for 32% of the time, Pallas kernels for 0%

profile of v1, /device:TPU:0, one launch (start us, length us, event | category | flops | bytes accessed | tf_op | source)
XLA Modules:
  0.0 569.8 jit_solution(4685522784400157122)
XLA Ops:
  32.4 5.8 %copy.330 = f32[2,2,1,256,1024]{3,0,2,1,4:T(2,128)} copy(f32[2,2,1,256,1024]{3,4,0,2,1:T(8,128)S(1)} %pad_maximum_fusion) | data formatting | bytes 8388608 | tf_op jit(solution)/shard_map/stack | solution.py:78
  38.2 5.0 all-to-all-start
  47.8 4.1 fusion.186
  51.9 40.2 %all-to-all-done = f32[2,2,1,256,1024]{3,0,2,1,4:T(2,128)} async-done(((f32[2,2,1,256,1024]{3,0,2,1,4:T(2,128)}), f32[2,2,1,256,1024]{3,0,2,1,4:T(2,128)}, u32[]{:S(2)}, u32[]{:S(2)}) %all-to-all-start) | async-done | bytes 4194336 | tf_op jit(solution)/shard_map/all_to_all | solution.py:135
  92.1 5.1 copy.331
  97.2 5.5 copy.332
  105.2 2.9 fusion.104
  108.1 2.9 fusion.102
  111.0 3.0 fusion.118
  114.0 3.7 subtract_bitcast_fusion.13
  120.3 2.6 subtract_bitcast_fusion.12
  126.7 2.6 add_bitcast_fusion.12
  131.7 2.9 fusion.88
  134.6 2.9 fusion.86
  137.4 3.0 fusion.124
  140.5 3.7 subtract_bitcast_fusion.11
  144.2 2.6 fusion.80
  146.8 2.6 subtract_bitcast_fusion.10
  153.2 2.8 add_bitcast_fusion.10
  157.6 5.2 copy.356
  162.7 4.8 all-to-all-start.1
  168.3 47.5 %all-to-all-done.1 = f32[2,2,1,1024,256]{4,0,2,1,3:T(2,128)} async-done(((f32[2,2,1,1024,256]{4,0,2,1,3:T(2,128)}), f32[2,2,1,1024,256]{4,0,2,1,3:T(2,128)}, u32[]{:S(2)}, u32[]{:S(2)}) %all-to-all-start.1) | async-done | bytes 4194336 | tf_op jit(solution)/shard_map/all_to_all | solution.py:140
  215.8 5.0 copy.357
  220.8 5.3 copy.358
  226.1 4.0 fusion.665
  234.4 3.7 reduce.2
  238.1 3.4 fusion.320
  255.0 3.7 add_bitcast_fusion.8
  258.6 3.7 reduce.3
  262.3 9.8 %fusion.192 = (f32[256,1024]{1,0:T(8,128)}, f32[256,1024]{1,0:T(8,128)}, f32[256,1024]{1,0:T(8,128)}, f32[256,1024]{1,0:T(8,128)}) fusion(f32[256,1024]{1,0:T(8,128)} %reduce.2, f32[]{:T(128)} %bitcast.53, f32[256,1024]{1,0:T(8,128)} %reduce.3), kind=kLoop, calls=%fused_computation.230 | loop fusion | flops 1572864 | bytes 6291460 | tf_op jit(solution)/shard_map/cos | solution.py:108
  282.9 2.9 copy.370
  285.8 4.8 fusion.316
  290.6 3.3 copy.369
  293.9 3.6 fusion.318
  314.1 3.2 copy.379
  317.4 50.7 %all_to_all.72 = f32[2,2,1,256,1024]{3,0,2,1,4:T(2,128)S(1)} all-to-all(f32[2,2,1,256,1024]{3,0,2,1,4:T(2,128)S(1)} %copy.379), channel_id=1, replica_groups=mesh['shot'=2,'row'=4,'freq'=4] {'row'}, dimensions={4} | all-to-all | bytes 8388608 | tf_op jit(solution)/shard_map/all_to_all | solution.py:135
  368.1 2.7 copy.380
  370.8 5.5 copy.381
  378.9 2.9 fusion.56
  381.8 2.9 fusion.54
  384.6 2.9 fusion.130
  387.6 3.8 subtract_bitcast_fusion.5
  396.6 2.6 subtract_bitcast_fusion.4
  400.4 2.6 add_bitcast_fusion.4
  405.1 2.9 fusion.40
  408.0 2.9 fusion.38
  410.9 3.0 fusion.136
  413.9 3.9 subtract_bitcast_fusion.3
  417.9 2.6 fusion.32
  423.1 2.6 subtract_bitcast_fusion.2
  426.9 2.8 add_bitcast_fusion.2
  431.3 5.3 copy.402
  436.6 5.0 all-to-all-start.3
  441.6 4.3 fusion.10
  449.7 40.1 %all-to-all-done.3 = f32[2,2,1,1024,256]{4,0,2,1,3:T(2,128)} async-done(((f32[2,2,1,1024,256]{4,0,2,1,3:T(2,128)}), f32[2,2,1,1024,256]{4,0,2,1,3:T(2,128)}, u32[]{:S(2)}, u32[]{:S(2)}) %all-to-all-start.3) | async-done | bytes 4194336 | tf_op jit(solution)/shard_map/all_to_all | solution.py:140
  489.8 5.0 copy.403
  494.8 5.2 copy.404
  500.1 4.6 fusion.663
  506.8 3.2 fusion.308
  523.1 2.8 subtract_bitcast_fusion
  532.7 3.0 pad_maximum_fusion.6
  535.8 2.9 copy.428
  538.6 4.5 fusion.14
  545.1 16.0 %reduce-scatter.5.cloned.1.call-done = f32[256,256]{0,1:T(8,128)} async-done(((f32[256,1024]{0,1:T(8,128)}), f32[256,256]{0,1:T(8,128)}) %reduce-scatter.5.cloned.1.call-update) | async-done | bytes 262160 | tf_op jit(solution)/shard_map/reduce_scatter | solution.py:144
  (135 shorter events, 135.6 us)
Async XLA Ops:
  8.9 1.6 copy-start.17
  38.2 5.1 copy-start.19
  38.2 7.0 %copy-start.18 = (f32[1,256,1024]{2,1,0:T(8,128)S(1)}, f32[1,256,1024]{2,1,0:T(8,128)}, u32[]{:S(2)}) copy-start(f32[1,256,1024]{2,1,0:T(8,128)} %param.7) | copy-start | bytes 3145732
  38.2 53.9 %all-to-all-start = ((f32[2,2,1,256,1024]{3,0,2,1,4:T(2,128)}), f32[2,2,1,256,1024]{3,0,2,1,4:T(2,128)}, u32[]{:S(2)}, u32[]{:S(2)}) async-start(f32[2,2,1,256,1024]{3,0,2,1,4:T(2,128)} %copy.330), calls=%async_computation | async-start | bytes 8388608 | tf_op jit(solution)/shard_map/all_to_all | solution.py:135
  43.2 191.2 %all-gather.5.cloned.1.call-start = ((), (), s32[]{:S(2)}) async-start(), calls=%async_computation.8 | async-start | bytes 5242880 | tf_op jit(solution)/shard_map/all_gather | solution.py:17
  51.9 79.1 %copy-start.7 = (f32[8,128,256]{2,1,0:T(8,128)}, f32[8,128,256]{2,1,0:T(8,128)S(1)}, u32[]{:S(2)}) copy-start(f32[8,128,256]{2,1,0:T(8,128)S(1)} %get-tuple-element.65) | copy-start | bytes 3145732
  162.7 53.1 %all-to-all-start.1 = ((f32[2,2,1,1024,256]{4,0,2,1,3:T(2,128)}), f32[2,2,1,1024,256]{4,0,2,1,3:T(2,128)}, u32[]{:S(2)}, u32[]{:S(2)}) async-start(f32[2,2,1,1024,256]{4,0,2,1,3:T(2,128)} %copy.356), calls=%async_computation.1 | async-start | bytes 8388608 | tf_op jit(solution)/shard_map/all_to_all | solution.py:140
  167.6 91.0 %all-gather.7.cloned.1.call-start = ((), (), s32[]{:S(2)}) async-start(), calls=%async_computation.9 | async-start | bytes 5242880 | tf_op jit(solution)/shard_map/all_gather | solution.py:17
  243.4 2.0 copy-start.3
  277.2 1.6 copy-start.1
  278.8 1.2 copy-start.9
  278.8 1.5 copy-start.11
  293.9 3.6 copy-start.2
  293.9 3.6 copy-start.13
  297.5 2.0 copy-start.6
  403.2 1.2 copy-start.8
  436.6 5.1 copy-start.10
  436.6 53.2 %all-to-all-start.3 = ((f32[2,2,1,1024,256]{4,0,2,1,3:T(2,128)}), f32[2,2,1,1024,256]{4,0,2,1,3:T(2,128)}, u32[]{:S(2)}, u32[]{:S(2)}) async-start(f32[2,2,1,1024,256]{4,0,2,1,3:T(2,128)} %copy.402), calls=%async_computation.3 | async-start | bytes 8388608 | tf_op jit(solution)/shard_map/all_to_all | solution.py:140
  441.6 103.5 %reduce-scatter.3.cloned.1.call-start = ((), (), s32[]{:S(2)}) async-start(), calls=%async_computation.6 | async-start | bytes 1310720 | tf_op jit(solution)/shard_map/reduce_scatter | solution.py:144
  446.0 1.3 copy-start.16
  447.2 1.2 copy-start.15
  447.2 113.8 %reduce-scatter.5.cloned.1.call-start = ((), (), s32[]{:S(2)}) async-start(), calls=%async_computation.7 | async-start | bytes 1310720 | tf_op jit(solution)/shard_map/reduce_scatter | solution.py:144
  506.8 3.2 copy-start.4
  512.3 1.9 copy-start.14
  514.2 2.0 copy-start.5
  525.9 2.3 copy-start.12
  528.2 2.5 copy-start
Sparse Core Ops, SparseCore 0:
  46.9 83.8 all-gather.4
  170.0 83.2 all-gather.6
  447.4 29.5 reduce-scatter.2
  532.9 28.1 reduce-scatter.4
